TPU v7x, 32 devices: a whole 2x2x4 slice. The times are simulated.
32 devices in a mesh: dp: 1, expert: 32 (over z, y, x, core).
Axes of the slice: x: 2, y: 2, z: 4, core: 2. Of those that a mesh axis runs over, the one named last changes fastest.
Arguments:
- out_grad: bfloat16 [4096, 3584], P(('dp', 'expert')), may hold values from -6 to 6
- inputs: bfloat16 [4096, 3584], P(('dp', 'expert')), may hold values from -6 to 6
- router_weight: float32 [3584, 32], P('expert'), may hold values from -0.09375 to 0.09375
- routes: int32 [4096, 8], P(('dp', 'expert')), may hold values from 0 to 31, all different within a row; in each aligned block of 128 rows (0 to 127, 128 to 255, ...) at most 40 rows name the same one
- saved_hidden: bfloat16 [40960, 1024], P(('dp', 'expert')), may hold values from -0.5 to 0.5
- down_weight: bfloat16 [32, 1024, 3584], P('expert', None, 'dp'), may hold values from -0.1875 to 0.1875
Outputs:
- hidden_grad: bfloat16 [40960, 1024], P(('dp', 'expert'))
- input_grad: bfloat16 [4096, 3584], P(('dp', 'expert'))
- gate_grad: float32 [4096, 8], P(('dp', 'expert'))
- router_grad: float32 [3584, 32], P('expert')
Inputs may be any that keep to these rules, and one draw needn't show every extreme that they name: `routes`: each row names 8 different experts. Within the rows of one device (aligned blocks of 128 rows) no expert is named by more than 40 rows, a bound that some block reaches.
All inputs are finite; a program needn't handle non-finite values.
Results may differ from a plain program's by a relative error of at most 0.0048.
Values may be sent and summed in bfloat16 or wider, within the bound.
A program may use at most 128 MiB of HBM per device.

v0:
```python
import jax
import jax.numpy as jnp
from jax import lax
from jax.sharding import PartitionSpec as P

ROUTE_SCALE = 2.5


def per_device(out_grad, inputs, router_weight, routes, saved_hidden, down_weight):
    precise = lax.Precision.HIGHEST
    experts = lax.axis_size("expert")
    tok_count, top_count = routes.shape
    slot_count = saved_hidden.shape[0]
    capacity = slot_count // experts
    model_width = out_grad.shape[1]
    rows_dev = router_weight.shape[0]
    router_full = lax.all_gather(router_weight, "expert", axis=0, tiled=True)
    inputs_wide = inputs.astype(jnp.float32)
    logits = jnp.dot(inputs_wide, router_full, precision=precise)
    scores = jax.nn.sigmoid(logits)
    expert_grid = jnp.arange(experts, dtype=jnp.int32)
    onehot = (routes[:, :, None] == expert_grid[None, None, :]).astype(jnp.float32)
    chosen = jnp.einsum("tke,te->tk", onehot, scores, precision=precise)
    totals = jnp.sum(chosen, axis=1, keepdims=True)
    gate_values = ROUTE_SCALE * chosen / totals
    flat_ids = routes.reshape(-1)
    flat_hot = (flat_ids[:, None] == expert_grid[None, :]).astype(jnp.int32)
    earlier = jnp.cumsum(flat_hot, axis=0) - flat_hot
    position = jnp.sum(earlier * flat_hot, axis=1)
    slot_index = flat_ids * capacity + position
    send_rows = (
        jnp.zeros((slot_count, model_width), jnp.bfloat16)
        .at[slot_index]
        .set(jnp.repeat(out_grad, top_count, axis=0))
    )
    send_gate = (
        jnp.zeros((slot_count,), jnp.bfloat16)
        .at[slot_index]
        .set(gate_values.reshape(-1).astype(jnp.bfloat16))
    )
    recv_rows, recv_gate = (
        lax.all_to_all(send_rows, "expert", split_axis=0, concat_axis=0, tiled=True),
        lax.all_to_all(send_gate, "expert", split_axis=0, concat_axis=0, tiled=True),
    )
    raw_grad = lax.dot_general(
        recv_rows,
        lax.all_gather(down_weight, "dp", axis=2, tiled=True)[0],
        (((1,), (1,)), ((), ())),
        preferred_element_type=jnp.float32,
    )
    gate_terms = jnp.sum(raw_grad * saved_hidden.astype(jnp.float32), axis=1)
    hidden_grad = (recv_gate.astype(jnp.float32)[:, None] * raw_grad).astype(jnp.bfloat16)
    returned = lax.all_to_all(gate_terms, "expert", split_axis=0, concat_axis=0, tiled=True)
    gate_grad = returned[slot_index].reshape(tok_count, top_count)
    weighted = jnp.sum(gate_grad * gate_values, axis=1, keepdims=True)
    chosen_grad = (ROUTE_SCALE * gate_grad - weighted) / totals * chosen * (1.0 - chosen)
    logit_grad = jnp.einsum("tke,tk->te", onehot, chosen_grad, precision=precise)
    input_grad = jnp.dot(logit_grad, router_full.T, precision=precise).astype(jnp.bfloat16)
    summed = lax.psum(jnp.dot(inputs_wide.T, logit_grad, precision=precise), ("dp", "expert"))
    router_grad = lax.dynamic_slice_in_dim(summed, lax.axis_index("expert") * rows_dev, rows_dev, 0)
    return (hidden_grad, input_grad, gate_grad, router_grad)


def solution(mesh):
    return jax.shard_map(
        per_device,
        mesh=mesh,
        in_specs=(
            P(("dp", "expert"), None),
            P(("dp", "expert"), None),
            P("expert", None),
            P(("dp", "expert"), None),
            P(("dp", "expert"), None),
            P("expert", None, "dp"),
        ),
        out_specs=(
            P(("dp", "expert"), None),
            P(("dp", "expert"), None),
            P(("dp", "expert"), None),
            P("expert", None),
        ),
        check_vma=False,
    )
```

profile of v0, /device:TPU:0, one launch (start us, length us, event | category | flops | bytes accessed | tf_op | source)
XLA Modules:
  0.0 474.0 jit_solution(943182720360045198)
XLA Ops:
  7.2 0.9 copy.24
  8.0 0.1 eq.42
  8.1 0.1 eq.38
  8.2 0.7 broadcast_multiply_fusion
  8.9 44.9 %all-gather = f32[32,112,32]{1,2,0:T(8,128)S(1)} all-gather(f32[1,112,32]{1,2,0:T(8,128)} %bitcast.64), channel_id=1, replica_groups=mesh['dp'=1,'expert'=32] {'expert'}, dimensions={0}, use_global_device_ids=true | all-gather | bytes 473088 | tf_op jit(solution)/shard_map/all_gather | solution.py:17
  53.8 0.3 copy.29
  54.1 0.3 reshape.107
  54.4 2.1 fusion.9
  56.6 0.1 copy.35
  56.7 0.6 fusion.11
  57.3 0.1 reduce_sum.40
  57.4 0.1 fusion.18
  57.5 0.1 reshape.94
  57.6 9.0 %reduce-window.6 = s32[32,8,128]{2,1,0:T(8,128)S(1)} reduce-window(s32[32,8,128]{2,1,0:T(8,128)S(1)} %fusion.17, s32[]{:T(128)} %constant.12.clone.1), window={size=1x1x128 pad=0_0x0_0x127_0}, to_apply=%region_0.0 | reduce-window | flops 4161536 | bytes 262148 | tf_op jit(solution)/shard_map/reduce-window
  66.7 0.1 slice.10
  66.8 0.1 copy.26
  66.9 0.1 copy.27
  67.0 0.1 broadcast_add_fusion
  67.1 0.1 copy.23
  67.2 0.1 mul.50
  67.4 7.6 %scatter_custom_fusion = bf16[1280]{0:T(1024)(128)(2,1)S(1)} fusion(s32[1024]{0:T(1024)S(1)} %bitcast.67, bf16[1024]{0:T(1024)(128)(2,1)S(1)} %reshape.94, bf16[]{:T(256)} %constant.10.clone.1), kind=kCustom, calls=%fused_computation.39 | custom fusion | bytes 2562 | tf_op jit(solution)/shard_map/scatter | solution.py:39
  75.0 0.7 all_to_all.30
  75.7 2.7 all-to-all-start
  78.4 15.3 %scatter_custom_fusion.1 = bf16[1280,3584]{1,0:T(8,128)(2,1)} fusion(s32[1024]{0:T(1024)S(1)} %bitcast.68, bf16[]{:T(256)} %constant.10.clone.1, bf16[128,3584]{1,0:T(8,128)(2,1)S(1)} %copy-done), kind=kCustom, calls=%fused_computation.5 | custom fusion | bytes 10092546 | tf_op jit(solution)/shard_map/scatter | solution.py:34
  93.7 6.0 %all-to-all-start.1 = ((bf16[32,40,3584]{2,1,0:T(8,128)(2,1)}), bf16[32,40,3584]{2,1,0:T(8,128)(2,1)}, u32[]{:S(2)}, u32[]{:S(2)}) async-start(bf16[32,40,3584]{2,1,0:T(8,128)(2,1)} %bitcast.55), calls=%async_computation.1 | async-start | bytes 18350080 | tf_op jit(solution)/shard_map/all_to_all | solution.py:42
  99.7 4.4 copy.31
  104.1 0.1 convert_reduce_fusion
  104.1 0.1 reshape.81
  104.2 198.5 %all-to-all-done.1 = bf16[32,40,3584]{2,1,0:T(8,128)(2,1)} async-done(((bf16[32,40,3584]{2,1,0:T(8,128)(2,1)}), bf16[32,40,3584]{2,1,0:T(8,128)(2,1)}, u32[]{:S(2)}, u32[]{:S(2)}) %all-to-all-start.1) | async-done | bytes 9175072 | tf_op jit(solution)/shard_map/all_to_all | solution.py:42
  302.7 16.2 %multiply_reduce_fusion = (f32[1280]{0:T(1024)S(1)}, bf16[1280,1024]{0,1:T(8,128)(2,1)}) fusion(bf16[1280,1024]{0,1:T(8,128)(2,1)} %copy.31, f32[1280]{0:T(1024)S(1)} %reshape.81, bf16[1280,3584]{1,0:T(8,128)(2,1)} %bitcast.10, bf16[1,1024,3584]{2,1,0:T(8,128)(2,1)} %param.11), kind=kOutput, calls=%fused_computation.7 | convolution fusion | flops 9401793536 | bytes 21768192 | tf_op jit(solution)/shard_map/dot_general | solution.py:45
  318.9 0.7 all_to_all.27
  319.6 2.5 all-to-all-start.2
  322.1 0.0 all-reduce.2.cloned.1.call-start
  322.2 4.4 copy.33
  326.6 2.6 all-to-all-done.2
  329.2 0.5 broadcast.79
  329.8 0.7 reduce.7
  330.5 0.1 all_to_all.29
  330.5 6.2 %gather_fusion = f32[1024]{0:T(1024)S(1)} fusion(f32[1280]{0:T(1024)S(1)} %all_to_all.29, s32[1024]{0:T(1024)S(1)} %broadcast_clamp_fusion), kind=kCustom, calls=%fused_computation | custom fusion | bytes 12288 | tf_op jit(solution)/shard_map/gather | solution.py:54
  336.7 0.1 reshape.80
  336.8 0.2 multiply_reduce_fusion.1
  337.0 0.7 copy.34
  337.6 0.1 subtract_multiply_fusion
  337.7 0.6 fusion.10
  338.4 1.3 convolution_bitcast_fusion
  339.7 2.5 convolution_convert_fusion
  342.2 123.5 %all-reduce.2.cloned.1.call-done = f32[3584,32]{0,1:T(8,128)} async-done(((f32[3584,32]{0,1:T(8,128)}), f32[3584,32]{0,1:T(8,128)}) %all-reduce.2.cloned.1.call-update) | async-done | bytes 458768 | tf_op jit(solution)/shard_map/psum | solution.py:59
  465.7 1.4 constant_dynamic-slice_fusion
  (12 shorter events, 0.1 us)
Async XLA Ops:
  7.2 71.3 %copy-start = (bf16[128,3584]{1,0:T(8,128)(2,1)S(1)}, bf16[128,3584]{1,0:T(8,128)(2,1)}, u32[]{:S(2)}) copy-start(bf16[128,3584]{1,0:T(8,128)(2,1)} %param.6) | copy-start | bytes 2752516
  75.7 18.0 %all-to-all-start = ((bf16[32,40,1]{1,2,0:T(2,128)(2,1)}), bf16[32,40,1]{1,2,0:T(2,128)(2,1)S(1)}, u32[]{:S(2)}, u32[]{:S(2)}) async-start(bf16[32,40,1]{1,2,0:T(2,128)(2,1)} %all_to_all.30), calls=%async_computation | async-start | bytes 32768 | tf_op jit(solution)/shard_map/all_to_all | solution.py:43
  93.7 209.1 %all-to-all-start.1 = ((bf16[32,40,3584]{2,1,0:T(8,128)(2,1)}), bf16[32,40,3584]{2,1,0:T(8,128)(2,1)}, u32[]{:S(2)}, u32[]{:S(2)}) async-start(bf16[32,40,3584]{2,1,0:T(8,128)(2,1)} %bitcast.55), calls=%async_computation.1 | async-start | bytes 18350080 | tf_op jit(solution)/shard_map/all_to_all | solution.py:42
  318.9 19.5 %copy-start.1 = (bf16[128,3584]{1,0:T(8,128)(2,1)S(1)}, bf16[128,3584]{1,0:T(8,128)(2,1)}, u32[]{:S(2)}) copy-start(bf16[128,3584]{1,0:T(8,128)(2,1)} %param.7) | copy-start | bytes 2752516
  319.6 9.7 %all-to-all-start.2 = ((f32[32,40,1]{1,2,0:T(1,128)}), f32[32,40,1]{1,2,0:T(1,128)S(1)}, u32[]{:S(2)}, u32[]{:S(2)}) async-start(f32[32,40,1]{1,2,0:T(1,128)} %bitcast.12), calls=%async_computation.2 | async-start | bytes 32768 | tf_op jit(solution)/shard_map/all_to_all | solution.py:53
  322.1 143.6 %all-reduce.2.cloned.1.call-start = ((), (), s32[]{:S(2)}) async-start(), calls=%async_computation.3 | async-start | bytes 917504 | tf_op jit(solution)/shard_map/psum | solution.py:59
Sparse Core Ops, SparseCore 0:
  339.9 125.8 all-reduce.1
where the time goes:
time: 475 us; the launch traced here: 474 us
  waiting for transfers between devices  325 us (68%)
  blocking collectives  44.9 us (9%)
  local copies, waits for them, and re-layouts  44.4 us (9%)
  matrix products  23.4 us (5%)
  between operations  14.2 us (3%)
  starting transfers between devices  11.3 us (2%)
  other arithmetic  11.1 us (2%)
    all_to_all x1, waiting for transfers between devices, per_device(): lax.all_to_all(send_rows, 'expert', split_axis=0, concat_axis=0, tiled=True)  199 us
    psum x1, waiting for transfers between devices, per_device(): lax.psum(jnp.dot(inputs_wide.T, logit_grad, precision=precise), ('dp', 'e...  123 us
    all_gather x1, blocking collectives, per_device(): router_full = lax.all_gather(router_weight, 'expert', axis=0, tiled=True)  44.9 us
    dot_general x1, matrix products, per_device(): lax.dot_general(recv_rows, lax.all_gather(down_weight, 'dp', axis=2, tile...  16.2 us
    scatter x1, local copies, waits for them, and re-layouts, per_device(): send_rows = jnp.zeros((slot_count, model_width), jnp.bfloat16).at[slot_in...  15.3 us
    unnamed x9, local copies, waits for them, and re-layouts  10.6 us
  transfers between devices with their start and end apart: 4, of which 3 were waited for; matrix products, arithmetic and copies ran while one was open for 6% of the time, Pallas kernels for 0%

commit v1 on v0

v1 whole, which is shorter than its diff:
```python
import jax
import jax.numpy as jnp
from jax import lax
from jax.experimental import pallas as pl
from jax.experimental.pallas import tpu as pltpu
from jax.sharding import PartitionSpec as P

ROUTE_SCALE = 2.5
MESH_ID = pl.DeviceIdType.MESH
UP, DOWN, XWAY, YWAY, PAIR, LOCAL = range(6)


def gather_kernel(rows_ref, weight_ref, rows_out, weight_out, send, recv, pair_recv, weight_send, weight_recv, own_sem):
    me = lax.axis_index("expert")
    core, x, y, z = me % 2, (me // 2) % 2, (me // 4) % 2, me // 8
    half = rows_ref.shape[0] // 2

    def number(xx, yy, zz, cc):
        return ((zz * 2 + yy) * 2 + xx) * 2 + cc

    barrier = pltpu.get_barrier_semaphore()

    def greet(i, carry):
        pl.semaphore_signal(barrier, inc=1, device_id={"expert": (me + i) % 32}, device_id_type=MESH_ID)
        return carry

    lax.fori_loop(1, 32, greet, 0)
    pl.semaphore_wait(barrier, 31)

    def weight_copy(to):
        return pltpu.make_async_remote_copy(
            src_ref=weight_ref, dst_ref=weight_out.at[me], send_sem=weight_send.at[to], recv_sem=weight_recv.at[me],
            device_id={"expert": to}, device_id_type=MESH_ID)

    def weight_arrival(source):
        return pltpu.make_async_remote_copy(
            src_ref=weight_ref, dst_ref=weight_out.at[source], send_sem=weight_send.at[source], recv_sem=weight_recv.at[source],
            device_id={"expert": source}, device_id_type=MESH_ID)

    def block(origin, part):
        return rows_out.at[origin, pl.ds(part * half, half)]

    def copy(origin, part, way, own=False):
        target = {
            UP: lambda: number(x, y, z + 1, core), DOWN: lambda: number(x, y, z - 1, core),
            XWAY: lambda: number(1 - x, y, z, core), YWAY: lambda: number(x, 1 - y, z, core),
            PAIR: lambda: number(x, y, z, 1 - core)}[way]()
        chip = origin // 2
        arrived = pair_recv if way == PAIR else recv
        return pltpu.make_async_remote_copy(
            src_ref=rows_ref.at[pl.ds(part * half, half)] if own else block(origin, part),
            dst_ref=block(origin, part), send_sem=send.at[way, chip, part], recv_sem=arrived.at[chip, part],
            device_id={"expert": target}, device_id_type=MESH_ID)

    def for_z(origin_step, act):
        if origin_step == 0:
            act()
        elif origin_step > 0:
            pl.when(z + origin_step <= 3)(act)
        else:
            pl.when(z + origin_step >= 0)(act)

    def along_z(step):
        own = step == 0

        def act():
            origin = number(x, y, z + step, core)
            for part in range(2):
                if not own:
                    copy(origin, part, XWAY).wait_recv()
                if step >= 0:
                    pl.when(z >= 1)(lambda: copy(origin, part, DOWN, own).start())
                if step <= 0:
                    pl.when(z <= 2)(lambda: copy(origin, part, UP, own).start())
                copy(origin, part, XWAY, own).start()
                copy(origin, part, YWAY, own).start()
                copy(origin, part, PAIR, own).start()

        for_z(step, act)

    def across(step):
        def act():
            from_x = number(1 - x, y, z + step, core)
            from_y = number(x, 1 - y, z + step, core)
            for part in range(2):
                copy(from_x, part, XWAY).wait_recv()
                if part == 0:
                    copy(from_x, part, YWAY).start()
                copy(from_x, part, PAIR).start()
                copy(from_y, part, YWAY).wait_recv()
                if part == 1:
                    copy(from_y, part, XWAY).start()
                copy(from_y, part, PAIR).start()

        for_z(step, act)

    def diagonal(step):
        def act():
            origin = number(1 - x, 1 - y, z + step, core)
            for part in range(2):
                copy(origin, part, XWAY).wait_recv()
                copy(origin, part, PAIR).start()

        for_z(step, act)

    def finish(step):
        def act():
            own = step == 0
            origin = number(x, y, z + step, core)
            for part in range(2):
                if step >= 0:
                    pl.when(z >= 1)(lambda: copy(origin, part, DOWN, own).wait_send())
                if step <= 0:
                    pl.when(z <= 2)(lambda: copy(origin, part, UP, own).wait_send())
                copy(origin, part, XWAY, own).wait_send()
                copy(origin, part, YWAY, own).wait_send()
            copy(number(1 - x, y, z + step, core), 0, YWAY).wait_send()
            copy(number(x, 1 - y, z + step, core), 1, XWAY).wait_send()

        for_z(step, act)

    own_copy = pltpu.make_async_copy(rows_ref, rows_out.at[me], own_sem.at[0])
    own_weight = pltpu.make_async_copy(weight_ref, weight_out.at[me], own_sem.at[1])

    def send_weight(i, carry):
        weight_copy((me + i) % 32).start()
        return carry

    lax.fori_loop(1, 32, send_weight, 0)
    along_z(0)
    own_copy.start()
    own_weight.start()
    for step in (1, -1):
        along_z(step)
    across(0)
    for step in (2, -2):
        along_z(step)
    for step in (1, -1):
        across(step)
    diagonal(0)
    for step in (3, -3):
        along_z(step)
    for step in (2, -2):
        across(step)
    for step in (1, -1):
        diagonal(step)
    for step in (3, -3):
        across(step)
    for step in (2, -2, 3, -3):
        diagonal(step)
    for step in (0, 1, -1, 2, -2, 3, -3):
        finish(step)
    own_copy.wait()
    own_weight.wait()

    def end_pair(i, carry):
        for part in range(2):
            copy(i * 2 + core, part, PAIR).wait_send()
            copy(i * 2 + 1 - core, part, PAIR).wait_recv()
        return carry

    lax.fori_loop(0, 16, end_pair, 0)

    def end_weight(i, carry):
        weight_copy((me + i) % 32).wait_send()
        weight_arrival((me + i) % 32).wait_recv()
        return carry

    lax.fori_loop(1, 32, end_weight, 0)


def gather_all(rows, weight):
    count = 32
    return pl.pallas_call(
        gather_kernel,
        out_shape=(
            jax.ShapeDtypeStruct((count,) + rows.shape, rows.dtype),
            jax.ShapeDtypeStruct((count,) + weight.shape, weight.dtype),
        ),
        in_specs=[pl.BlockSpec(memory_space=pltpu.VMEM)] * 2,
        out_specs=(pl.BlockSpec(memory_space=pl.ANY), pl.BlockSpec(memory_space=pl.ANY)),
        scratch_shapes=[
            pltpu.SemaphoreType.DMA((5, 16, 2)),
            pltpu.SemaphoreType.DMA((16, 2)),
            pltpu.SemaphoreType.DMA((16, 2)),
            pltpu.SemaphoreType.DMA((32,)),
            pltpu.SemaphoreType.DMA((32,)),
            pltpu.SemaphoreType.DMA((2,)),
        ],
        compiler_params=pltpu.CompilerParams(collective_id=0, has_side_effects=True),
    )(rows, weight)


def dispatched(out_grad, slot_of, send_gate, capacity):
    experts, tok_count = slot_of.shape
    pick = (slot_of[:, None, :] == jnp.arange(capacity, dtype=jnp.float32)[None, :, None]).astype(jnp.bfloat16)
    rows = jnp.einsum("ect,td->ecd", pick, out_grad, preferred_element_type=jnp.float32).astype(jnp.bfloat16)
    return lax.all_to_all(rows.reshape(experts * capacity, -1), "expert", split_axis=0, concat_axis=0, tiled=True)


def per_device(use_gather, out_grad, inputs, router_weight, routes, saved_hidden, down_weight):
    precise = lax.Precision.HIGHEST
    experts = lax.axis_size("expert")
    tok_count, top_count = routes.shape
    slot_count = saved_hidden.shape[0]
    capacity = slot_count // experts
    model_width = out_grad.shape[1]
    rows_dev = router_weight.shape[0]
    if use_gather:
        all_rows, router_full = gather_all(out_grad, router_weight.reshape(-1, 128))
        router_full = router_full.reshape(model_width, experts)
    else:
        router_full = lax.all_gather(router_weight, "expert", axis=0, tiled=True)
    inputs_wide = inputs.astype(jnp.float32)
    logits = jnp.dot(inputs_wide, router_full, precision=precise)
    scores = jax.nn.sigmoid(logits)
    expert_grid = jnp.arange(experts, dtype=jnp.int32)
    named = routes[:, :, None] == expert_grid[None, None, :]
    hot = jnp.any(named, axis=1)
    chosen = jnp.where(hot, scores, 0.0)
    totals = jnp.sum(chosen, axis=1, keepdims=True)
    gates = ROUTE_SCALE * chosen / totals
    token_grid = jnp.arange(tok_count)
    before = (token_grid[None, :] < token_grid[:, None]).astype(jnp.bfloat16)
    position = jnp.dot(before, hot.astype(jnp.bfloat16), preferred_element_type=jnp.float32)
    position = jnp.where(hot, position, -1.0)
    sent = jnp.stack([position.T, gates.astype(jnp.bfloat16).astype(jnp.float32).T], axis=1)
    got = lax.all_to_all(sent, "expert", split_axis=0, concat_axis=0, tiled=True)
    pick_slot, pick_gate = got[:, 0], got[:, 1]
    pick = pick_slot[:, None, :] == jnp.arange(capacity, dtype=jnp.float32)[None, :, None]
    if use_gather:
        rows = jnp.einsum("sct,std->scd", pick.astype(jnp.bfloat16), all_rows, preferred_element_type=jnp.float32)
        rows = rows.astype(jnp.bfloat16).reshape(slot_count, model_width)
    else:
        rows = dispatched(out_grad, position.T, None, capacity)
    slot_gate = jnp.sum(jnp.where(pick, pick_gate[:, None, :], 0.0), axis=2)
    raw_grad = lax.dot_general(
        rows,
        lax.all_gather(down_weight, "dp", axis=2, tiled=True)[0],
        (((1,), (1,)), ((), ())),
        preferred_element_type=jnp.float32,
    )
    gate_terms = jnp.sum(raw_grad * saved_hidden.astype(jnp.float32), axis=1)
    hidden_grad = (slot_gate.reshape(-1)[:, None] * raw_grad).astype(jnp.bfloat16)
    back = jnp.sum(jnp.where(pick, gate_terms.reshape(experts, capacity)[:, :, None], 0.0), axis=1)
    returned = lax.all_to_all(back, "expert", split_axis=0, concat_axis=0, tiled=True).T
    gate_grad = jnp.sum(jnp.where(named, returned[:, None, :], 0.0), axis=2)
    weighted = jnp.sum(returned * gates, axis=1, keepdims=True)
    logit_grad = jnp.where(hot, (ROUTE_SCALE * returned - weighted) / totals * chosen * (1.0 - chosen), 0.0)
    input_grad = jnp.dot(logit_grad, router_full.T, precision=precise).astype(jnp.bfloat16)
    part = jnp.dot(inputs_wide.T, logit_grad, precision=precise)
    terms = lax.all_to_all(part.reshape(experts, -1, 128), "expert", split_axis=0, concat_axis=0, tiled=True)
    router_grad = lax.psum(jnp.sum(terms, axis=0).reshape(rows_dev, experts), "dp")
    return (hidden_grad, input_grad, gate_grad, router_grad)


def solution(mesh):
    use_gather = mesh.shape["expert"] == 32 and mesh.shape["dp"] == 1

    def run(*args):
        return per_device(use_gather, *args)

    return jax.shard_map(
        run,
        mesh=mesh,
        in_specs=(
            P(("dp", "expert"), None),
            P(("dp", "expert"), None),
            P("expert", None),
            P(("dp", "expert"), None),
            P(("dp", "expert"), None),
            P("expert", None, "dp"),
        ),
        out_specs=(
            P(("dp", "expert"), None),
            P(("dp", "expert"), None),
            P(("dp", "expert"), None),
            P("expert", None),
        ),
        check_vma=False,
    )
```

time: 475 us -> 222 us (0.47)
  waiting for transfers between devices: 325 us -> 13.2 us
  Pallas kernels: 0 us -> 138 us
  blocking collectives: 44.9 us -> 0 us
  local copies, waits for them, and re-layouts: 44.4 us -> 17.8 us
  between operations: 14.2 us -> 0.73 us
  matrix products: 23.4 us -> 36.8 us
    all_to_all x3, waiting for transfers between devices: 201 us -> 13.2 us  [the longest x1 7.02 us: per_device(): lax.all_to_all(back, 'expert', split_axis=0, concat_axis=0, tiled=True)]
    pallas_call x0 -> x1, Pallas kernels: none -> 138 us  [gather_all(): pl.pallas_call(gather_kernel, out_shape=(jax.ShapeDtypeStruct((count,) +...]
    psum x1 -> x0, waiting for transfers between devices: 123 us -> none  [per_device(): lax.psum(jnp.dot(inputs_wide.T, logit_grad, precision=precise), ('dp', 'e...]
    all_gather x1 -> x0, blocking collectives: 44.9 us -> none  [per_device(): router_full = lax.all_gather(router_weight, 'expert', axis=0, tiled=True)]
    scatter x2 -> x0, local copies, waits for them, and re-layouts: 22.8 us -> none  [the longest x1 15.3 us: per_device(): send_rows = jnp.zeros((slot_count, model_width), jnp.bfloat16).at[slot_in...]
    dot_general x4, matrix products: 18.7 us -> 32.4 us  [the longest x1 16.5 us: per_device(): lax.dot_general(rows, lax.all_gather(down_weight, 'dp', axis=2, tiled=Tru...]
    another operation x3 -> x2, other arithmetic: 9.15 us -> 0.01 us  [per_device(): jnp.stack([position.T, gates.astype(jnp.bfloat16).astype(jnp.float32).T],...]
    gather x1 -> x0, local copies, waits for them, and re-layouts: 6.15 us -> none  [per_device(): gate_grad = returned[slot_index].reshape(tok_count, top_count)]
  transfers between devices with their start and end apart: 4 -> 3, of which waited for: 3 -> 3; matrix products, arithmetic and copies ran while one was open for 6% -> 7% of each run, Pallas kernels for 0% -> 0%
where the time goes in v1:
time: 222 us
  Pallas kernels  138 us (62%)
  matrix products  36.8 us (17%)
  local copies, waits for them, and re-layouts  17.8 us (8%)
  waiting for transfers between devices  13.2 us (6%)
  starting transfers between devices  8.32 us (4%)
  other arithmetic  6.76 us (3%)
    pallas_call x1, Pallas kernels, gather_all(): pl.pallas_call(gather_kernel, out_shape=(jax.ShapeDtypeStruct((count,) +...  138 us
    dot_general x1, matrix products, per_device(): lax.dot_general(rows, lax.all_gather(down_weight, 'dp', axis=2, tiled=Tru...  16.5 us
    dot_general x1, matrix products, per_device(): jnp.einsum('sct,std->scd', pick.astype(jnp.bfloat16), all_rows, preferred...  15.3 us
    unnamed x8, local copies, waits for them, and re-layouts  10.3 us
    all_to_all x1, waiting for transfers between devices, per_device(): lax.all_to_all(back, 'expert', split_axis=0, concat_axis=0, tiled=True)  7.02 us
  transfers between devices with their start and end apart: 3, of which 3 were waited for; matrix products, arithmetic and copies ran while one was open for 7% of the time, Pallas kernels for 0%

profile of v1, /device:TPU:0, one launch (start us, length us, event | category | flops | bytes accessed | tf_op | source)
XLA Modules:
  0.0 221.7 jit_solution(4237631635191224121)
XLA Ops:
  0.6 0.0 copy-start
  0.6 0.8 fusion.7
  1.4 0.8 copy.30
  2.2 0.7 reshape.31.weight_ref
  2.9 138.1 %shard_map.93 = (bf16[32,128,3584]{2,1,0:T(8,128)(2,1)}, f32[32,28,128]{2,1,0:T(8,128)}) custom-call(bf16[128,3584]{1,0:T(8,128)(2,1)} %rows_ref.1, f32[28,128]{1,0:T(8,128)} %reshape.31.weight_ref), custom_call_target="tpu_custom_call" | custom-call | tf_op jit(solution)/shard_map/pallas_call | solution.py:174
  141.0 1.6 reshape.32
  142.6 0.1 fusion.5
  142.7 0.0 copy-done
  142.7 1.6 fusion.8
  144.4 0.6 copy.31
  145.0 2.6 %all-to-all-start = ((f32[32,2,128]{2,1,0:T(2,128)}), f32[32,2,128]{2,1,0:T(2,128)S(1)}, u32[]{:S(2)}, u32[]{:S(2)}) async-start(f32[32,2,128]{2,1,0:T(2,128)} %copy.31), calls=%async_computation | async-start | bytes 65536 | tf_op jit(solution)/shard_map/all_to_all | solution.py:228
  147.6 4.4 %copy.32 = bf16[1280,1024]{0,1:T(8,128)(2,1)} copy(bf16[1280,1024]{1,0:T(8,128)(2,1)} %param.10) | data formatting | bytes 5242880 | tf_op args[4]
  152.0 2.9 %all-to-all-done = f32[32,2,128]{2,1,0:T(2,128)S(1)} async-done(((f32[32,2,128]{2,1,0:T(2,128)}), f32[32,2,128]{2,1,0:T(2,128)S(1)}, u32[]{:S(2)}, u32[]{:S(2)}) %all-to-all-start) | async-done | bytes 32800 | tf_op jit(solution)/shard_map/all_to_all | solution.py:228
  154.9 15.3 %convolution_convert_fusion = bf16[32,40,3584]{2,1,0:T(8,128)(2,1)} fusion(bf16[32,128,3584]{2,1,0:T(8,128)(2,1)} %get-tuple-element.7, f32[32,128]{1,0:T(8,128)S(1)} %bitcast.46), kind=kOutput, calls=%fused_computation | convolution fusion | flops 1179156480 | bytes 38551552 | tf_op jit(solution)/shard_map/sct,std->scd/dot_general | solution.py:232
  170.2 16.5 %multiply_reduce_fusion = (f32[1280]{0:T(1024)S(1)}, f32[1280,1024]{0,1:T(8,128)}) fusion(bf16[1280,1024]{0,1:T(8,128)(2,1)} %copy.32, bf16[1280,3584]{1,0:T(8,128)(2,1)} %bitcast.41, bf16[1,1024,3584]{2,1,0:T(8,128)(2,1)} %param.11), kind=kOutput, calls=%fused_computation.3 | convolution fusion | flops 9399172096 | bytes 24384512 | tf_op jit(solution)/shard_map/dot_general | solution.py:237
  186.7 0.1 broadcast_in_dim.62
  186.8 0.9 select_reduce_fusion
  187.7 3.0 %all-to-all-start.1 = ((f32[32,1,128]{2,1,0:T(1,128)}), f32[32,1,128]{2,1,0:T(1,128)S(1)}, u32[]{:S(2)}, u32[]{:S(2)}) async-start(f32[32,1,128]{2,1,0:T(1,128)} %bitcast.8), calls=%async_computation.1 | async-start | bytes 32768 | tf_op jit(solution)/shard_map/all_to_all | solution.py:246
  190.6 0.1 mul.32
  190.7 7.0 %all-to-all-done.1 = f32[32,1,128]{2,1,0:T(1,128)S(1)} async-done(((f32[32,1,128]{2,1,0:T(1,128)}), f32[32,1,128]{2,1,0:T(1,128)S(1)}, u32[]{:S(2)}, u32[]{:S(2)}) %all-to-all-start.1) | async-done | bytes 16416 | tf_op jit(solution)/shard_map/all_to_all | solution.py:246
  197.8 0.5 convolution_bitcast_fusion
  198.2 1.8 copy.33
  200.0 2.7 %reshape.34 = f32[32,28,128]{2,1,0:T(8,128)} reshape(f32[3584,32]{1,0:T(8,128)} %copy.33) | data formatting | bytes 917504 | tf_op jit(solution)/shard_map/reshape | solution.py:252
  202.7 2.8 %all-to-all-start.2 = ((f32[32,28,128]{2,1,0:T(8,128)}), f32[32,28,128]{2,1,0:T(8,128)S(1)}, u32[]{:S(2)}, u32[]{:S(2)}) async-start(f32[32,28,128]{2,1,0:T(8,128)} %reshape.34), calls=%async_computation.2 | async-start | bytes 1048576 | tf_op jit(solution)/shard_map/all_to_all | solution.py:252
  205.5 0.0 copy-start.1
  205.5 4.4 %multiply_convert_fusion = bf16[1280,1024]{0,1:T(8,128)(2,1)} fusion(f32[1280,1024]{0,1:T(8,128)} %get-tuple-element.31, f32[1280]{0:T(1024)S(1)} %mul.32), kind=kLoop, calls=%fused_computation.4 | loop fusion | flops 2621440 | bytes 7869440 | tf_op jit(solution)/shard_map/convert_element_type | solution.py:244
  209.9 4.4 %copy.34 = bf16[1280,1024]{1,0:T(8,128)(2,1)} copy(bf16[1280,1024]{0,1:T(8,128)(2,1)} %multiply_convert_fusion) | data formatting | bytes 5242880
  214.3 0.0 copy-done.1
  214.3 0.6 select_reduce_fusion.2
  214.9 2.7 %convolution_convert_fusion.1 = bf16[128,3584]{1,0:T(8,128)(2,1)} fusion(f32[3584,32]{1,0:T(8,128)S(1)} %reshape.32, pred[128,32]{0,1:T(8,128)(4,1)S(1)} %fusion.7, f32[128,32]{0,1:T(8,128)S(1)} %bitcast.45, f32[32,128]{1,0:T(8,128)S(1)} %get-tuple-element.29, f32[128]{0:T(128)S(1)} %multiply_reduce_fusion.1, f32[128]{0:T(128)S(1)} %get-tuple-element.28), kind=kOutput, calls=%fused_computation.5 | convolution fusion | flops 176652288 | bytes 1414144 | tf_op jit(solution)/shard_map/dot_general | solution.py:250
  217.6 3.3 %all-to-all-done.2 = f32[32,28,128]{2,1,0:T(8,128)S(1)} async-done(((f32[32,28,128]{2,1,0:T(8,128)}), f32[32,28,128]{2,1,0:T(8,128)S(1)}, u32[]{:S(2)}, u32[]{:S(2)}) %all-to-all-start.2) | async-done | bytes 458784 | tf_op jit(solution)/shard_map/all_to_all | solution.py:252
  220.9 0.1 reshape.35
  221.0 0.7 copy.35
  (5 shorter events, 0.1 us)
Async XLA Ops:
  0.6 142.1 %copy-start = (bf16[128,3584]{1,0:T(8,128)(2,1)S(1)}, bf16[128,3584]{1,0:T(8,128)(2,1)}, u32[]{:S(2)}) copy-start(bf16[128,3584]{1,0:T(8,128)(2,1)} %param.7) | copy-start | bytes 2752516
  145.0 9.8 %all-to-all-start = ((f32[32,2,128]{2,1,0:T(2,128)}), f32[32,2,128]{2,1,0:T(2,128)S(1)}, u32[]{:S(2)}, u32[]{:S(2)}) async-start(f32[32,2,128]{2,1,0:T(2,128)} %copy.31), calls=%async_computation | async-start | bytes 65536 | tf_op jit(solution)/shard_map/all_to_all | solution.py:228
  187.7 10.1 %all-to-all-start.1 = ((f32[32,1,128]{2,1,0:T(1,128)}), f32[32,1,128]{2,1,0:T(1,128)S(1)}, u32[]{:S(2)}, u32[]{:S(2)}) async-start(f32[32,1,128]{2,1,0:T(1,128)} %bitcast.8), calls=%async_computation.1 | async-start | bytes 32768 | tf_op jit(solution)/shard_map/all_to_all | solution.py:246
  202.7 18.2 %all-to-all-start.2 = ((f32[32,28,128]{2,1,0:T(8,128)}), f32[32,28,128]{2,1,0:T(8,128)S(1)}, u32[]{:S(2)}, u32[]{:S(2)}) async-start(f32[32,28,128]{2,1,0:T(8,128)} %reshape.34), calls=%async_computation.2 | async-start | bytes 1048576 | tf_op jit(solution)/shard_map/all_to_all | solution.py:252
  205.5 8.8 %copy-start.1 = (s32[128,8]{0,1:T(8,128)S(1)}, s32[128,8]{0,1:T(8,128)}, u32[]{:S(2)}) copy-start(s32[128,8]{0,1:T(8,128)} %param.9) | copy-start | bytes 12292
